TPU v7x, 32 devices: a whole 2x2x4 slice. The times are simulated.
32 devices in a mesh: grp: 16 (over z, x, core), slab: 2 (over y).
Axes of the slice: x: 2, y: 2, z: 4, core: 2. Of those that a mesh axis runs over, the one named last changes fastest.
Arguments:
- ligand_grids: float32 [2, 4, 128, 128, 128], P(None, None, 'grp', 'slab'), may hold values from -6 to 6
- receptor_kernel: bfloat16 [16, 2, 2, 128, 128, 128], P('grp', None, None, 'slab'), may hold values from -3 to 3
Outputs:
- best_score: bfloat16 [16, 128, 128, 128], P('grp', None, 'slab')
All inputs are finite; a program needn't handle non-finite values.
Results may differ from a plain program's by a relative error of at most 0.018.
Values may be sent and summed in bfloat16 or wider, within the bound.
A program may use at most 128 MiB of HBM per device.

v0:
```python
import math
import jax
import jax.numpy as jnp
from jax import lax
from jax.sharding import PartitionSpec as P

highest = lax.Precision.HIGHEST


def coefficients(length, inverse):
    positions = jnp.arange(length, dtype=jnp.int32)
    phases = positions[:, None] * positions[None, :] % length
    angles = phases.astype(jnp.float32) * (2.0 * math.pi / length)
    scaling = 1.0 / math.sqrt(length)
    cosine = jnp.cos(angles) * scaling
    sine_part = jnp.sin(angles) * scaling
    if inverse:
        sine_part = -sine_part
    upper_rows = jnp.stack([cosine, sine_part])
    lower_rows = jnp.stack([-sine_part, cosine])
    return jnp.stack([upper_rows, lower_rows])


def pack_pairs(ligand_piece):
    stacked = jnp.stack([ligand_piece[:, 0::2], ligand_piece[:, 1::2]])
    return stacked.reshape((2, stacked.shape[1] * stacked.shape[2]) + stacked.shape[3:])


def body(ligand_grids, receptor_kernel):
    length = ligand_grids.shape[4]
    rotations = ligand_grids.shape[0]
    channel_pairs = ligand_grids.shape[1] // 2
    forward = coefficients(length, False)
    forward_low = forward.astype(jnp.bfloat16)
    inverse_low = coefficients(length, True).astype(jnp.bfloat16)
    packed = pack_pairs(ligand_grids)
    lines = jnp.einsum("pqkn,qrzxn->pkrzx", forward, packed, precision=highest)
    columns = lax.all_to_all(
        lines.astype(jnp.bfloat16), "grp", split_axis=1, concat_axis=3, tiled=True
    ).astype(lines.dtype)
    partial_value = jnp.einsum("pqkn,qyrnx->pyrkx", forward, columns, precision=highest).astype(
        jnp.bfloat16
    )
    pieces = jnp.einsum(
        "pqkn,qyrzn->pyrzk",
        forward_low,
        lax.all_to_all(partial_value, "slab", split_axis=3, concat_axis=4, tiled=True),
        preferred_element_type=jnp.float32,
    ).astype(jnp.bfloat16)
    collected = lax.all_gather(pieces, "grp", axis=1, tiled=True)
    spectrum = jnp.transpose(collected, (0, 2, 3, 4, 1))
    spec_split = spectrum.reshape((2, rotations, channel_pairs) + spectrum.shape[2:])
    kernel_one = receptor_kernel[0]
    kernel_real = kernel_one[0][None].astype(jnp.float32)
    kernel_imag = kernel_one[1][None].astype(jnp.float32)
    spec_real = spec_split[0].astype(jnp.float32)
    spec_imag = spec_split[1].astype(jnp.float32)
    real_part = jnp.sum(kernel_real * spec_real - kernel_imag * spec_imag, axis=1)
    imag_part = jnp.sum(kernel_real * spec_imag + kernel_imag * spec_real, axis=1)
    product = jnp.stack([real_part, imag_part]).astype(jnp.bfloat16)
    rows_done = jnp.einsum(
        "pqkn,qrznm->przkm", inverse_low, product, preferred_element_type=jnp.float32
    ).astype(jnp.bfloat16)
    planes = jnp.einsum(
        "pqkn,qrzxn->przxk", inverse_low, rows_done, preferred_element_type=jnp.float32
    ).astype(jnp.bfloat16)
    scores = jnp.einsum(
        "qkn,qrnxy->rkxy",
        inverse_low[0],
        lax.all_to_all(planes, "slab", split_axis=3, concat_axis=2, tiled=True),
        preferred_element_type=jnp.float32,
    )
    return jnp.max(scores, axis=0).astype(jnp.bfloat16)[None]


def solution(mesh):
    return jax.shard_map(
        body,
        mesh=mesh,
        in_specs=(P(None, None, "grp", "slab", None), P("grp", None, None, "slab", None, None)),
        out_specs=P("grp", None, "slab", None),
        check_vma=False,
    )
```

profile of v0, /device:TPU:0, one launch (start us, length us, event | category | flops | bytes accessed | tf_op | source)
XLA Modules:
  0.0 428.6 jit_solution(18179298888462412341)
XLA Ops:
  6.5 0.3 sine_multiply_fusion
  7.1 1.7 fusion.59
  8.8 1.8 bitcast_convert_fusion.6
  10.6 3.0 copy.32
  13.6 1.5 reshape.162
  15.1 31.9 %all_to_all.54 = bf16[16,2,16384]{2,1,0:T(2,128)(2,1)S(1)} all-to-all(bf16[16,2,16384]{2,1,0:T(2,128)(2,1)S(1)} %reshape.162), channel_id=1, replica_groups=mesh['grp'=16,'slab'=2] {'grp'}, dimensions={0} | all-to-all | bytes 2097152 | tf_op jit(solution)/shard_map/all_to_all | solution.py:38
  47.0 1.3 reshape.163
  48.3 3.0 fusion.26
  51.3 4.8 %copy.36 = bf16[2,8,4,128,64]{4,0,2,1,3:T(2,128)(2,1)S(1)} copy(bf16[2,8,4,128,64]{3,4,0,2,1:T(8,128)(2,1)} %fusion.26) | data formatting | bytes 2097152 | tf_op jit(solution)/shard_map/convert_element_type | solution.py:41
  56.1 1.6 reshape.164
  57.8 18.4 %all_to_all.55 = bf16[2,2,131072]{2,1,0:T(2,128)(2,1)} all-to-all(bf16[2,2,131072]{2,1,0:T(2,128)(2,1)S(1)} %reshape.164), channel_id=1, replica_groups=mesh['grp'=16,'slab'=2] {'slab'}, dimensions={0} | all-to-all | bytes 2097152 | tf_op jit(solution)/shard_map/all_to_all | solution.py:47
  76.2 2.6 reshape.165
  78.8 3.5 copy.90
  82.3 3.9 reshape.151
  86.2 0.5 fusion.29
  86.7 1.1 copy.38
  87.8 11.8 %bitcast_convert_fusion.3 = (f32[2,64,128,128]{3,2,1,0:T(8,128)}, f32[2,64,128,128]{3,2,1,0:T(8,128)}) fusion(bf16[1,2,2,64,128,128]{5,4,3,2,1,0:T(8,128)(2,1)} %param.3), kind=kLoop, calls=%fused_computation.25 | loop fusion | flops 4194304 | bytes 25165824 | tf_op jit(solution)/shard_map/convert_element_type | solution.py:54
  99.5 8.7 %copy.31 = f32[2,64,128,128]{2,1,0,3:T(8,128)} copy(f32[2,64,128,128]{3,2,1,0:T(8,128)} %get-tuple-element.9) | data formatting | bytes 16777216 | tf_op jit(solution)/shard_map/convert_element_type | solution.py:54
  108.3 8.8 %copy.39 = f32[2,64,128,128]{2,1,0,3:T(8,128)} copy(f32[2,64,128,128]{3,2,1,0:T(8,128)} %get-tuple-element.10) | data formatting | bytes 16777216 | tf_op jit(solution)/shard_map/convert_element_type | solution.py:55
  117.3 0.3 fusion.48
  117.6 95.5 %all-gather.2.cloned.1.call-done = bf16[2,128,4,64,128]{4,3,2,0,1:T(8,128)(2,1)} async-done(((bf16[2,8,4,64,128]{4,3,2,0,1:T(8,128)(2,1)}), bf16[2,128,4,64,128]{4,3,2,0,1:T(8,128)(2,1)}) %all-gather.2.cloned.1.call-update) | async-done | bytes 16777232 | tf_op jit(solution)/shard_map/all_gather | solution.py:50
  213.2 15.2 %fusion.58 = (bf16[1,4,64,128,128]{3,2,1,0,4:T(8,128)(2,1)}, bf16[1,4,64,128,128]{3,2,1,0,4:T(8,128)(2,1)}) fusion(bf16[2,4,64,128,128]{3,2,1,0,4:T(8,128)(2,1)} %bitcast.146), kind=kLoop, calls=%fused_computation.75 | loop fusion | bytes 33554432 | tf_op jit(solution)/shard_map/slice | solution.py:56
  228.4 17.3 %fusion.1 = (bf16[2,64,128,128]{2,1,0,3:T(8,128)(2,1)}, bf16[2,64,128,128]{2,1,0,3:T(8,128)(2,1)}) fusion(bf16[2,2,64,128,128]{3,2,1,0,4:T(8,128)(2,1)} %bitcast.144, bf16[2,2,64,128,128]{3,2,1,0,4:T(8,128)(2,1)} %bitcast.143, f32[2,64,128,128]{2,1,0,3:T(8,128)} %copy.39, f32[2,64,128,128]{2,1,0,3:T(8,128)S(1)} %copy-done), kind=kLoop, calls=%fused_computation.5 | loop fusion | flops 37748736 | bytes 41943040 | tf_op jit(solution)/shard_map/reduce_sum | solution.py:58
  245.7 7.0 %copy.88 = bf16[2,64,128,128]{2,3,1,0:T(8,128)(2,1)} copy(bf16[2,64,128,128]{2,1,0,3:T(8,128)(2,1)} %get-tuple-element.5) | data formatting | bytes 8388608 | tf_op jit(solution)/shard_map/reduce_sum | solution.py:58
  252.6 4.6 %copy.89 = bf16[2,64,128,128]{2,3,1,0:T(8,128)(2,1)} copy(bf16[2,64,128,128]{2,1,0,3:T(8,128)(2,1)S(1)} %copy-done.1) | data formatting | bytes 8388608 | tf_op jit(solution)/shard_map/reduce_sum | solution.py:59
  257.3 9.3 %fusion.7 = bf16[2,2,64,128,128]{4,3,0,2,1:T(8,128)(2,1)} fusion(bf16[1,2,64,128,128]{3,4,0,2,1:T(8,128)(2,1)} %bitcast.153, bf16[1,2,64,128,128]{3,4,0,2,1:T(8,128)(2,1)} %bitcast.152, bf16[1,2,128,128]{3,2,1,0:T(8,128)(2,1)S(1)} %get-tuple-element.16, bf16[1,2,128,128]{3,2,1,0:T(8,128)(2,1)S(1)} %get-tuple-element.15), kind=kOutput, calls=%fused_computation.12 | convolution fusion | flops 4320657408 | bytes 16908288 | tf_op jit(solution)/shard_map/pqkn,qrzxn->przxk/dot_general | solution.py:64
  266.6 12.2 %copy.43 = bf16[2,2,64,128,128]{4,0,2,1,3:T(2,128)(2,1)S(1)} copy(bf16[2,2,64,128,128]{4,3,0,2,1:T(8,128)(2,1)} %fusion.7) | data formatting | bytes 16777216 | tf_op jit(solution)/shard_map/convert_element_type | solution.py:66
  278.8 97.3 %all_to_all.56 = bf16[2,2,64,128,128]{4,0,2,1,3:T(2,128)(2,1)} all-to-all(bf16[2,2,64,128,128]{4,0,2,1,3:T(2,128)(2,1)S(1)} %copy.43), channel_id=1, replica_groups=mesh['grp'=16,'slab'=2] {'slab'}, dimensions={3} | all-to-all | bytes 16777216 | tf_op jit(solution)/shard_map/all_to_all | solution.py:70
  376.1 12.0 %copy.44 = bf16[2,2,64,128,128]{4,3,2,1,0:T(8,128)(2,1)} copy(bf16[2,2,64,128,128]{4,0,2,1,3:T(2,128)(2,1)} %all_to_all.56) | data formatting | bytes 16777216 | tf_op jit(solution)/shard_map/all_to_all | solution.py:70
  388.1 9.4 %copy.45 = bf16[2,2,2,64,64,128]{5,4,3,2,1,0:T(8,128)(2,1)} copy(bf16[2,2,2,64,64,128]{5,4,2,3,1,0:T(8,128)(2,1)} %bitcast.145) | data formatting | bytes 16777216 | tf_op jit(solution)/shard_map/all_to_all | solution.py:70
  397.5 21.2 %bitcast_reduce_fusion = bf16[64,128,128]{2,1,0:T(8,128)(2,1)S(1)} fusion(bf16[2,2,128,64,128]{4,3,2,1,0:T(8,128)(2,1)} %bitcast.149, bf16[1,128,128]{2,1,0:T(8,128)(2,1)S(1)} %get-tuple-element.20, bf16[1,128,128]{2,1,0:T(8,128)(2,1)S(1)} %fusion.51), kind=kOutput, calls=%fused_computation.17 | convolution fusion | flops 1074823168 | bytes 10551296 | tf_op jit(solution)/shard_map/qkn,qrnxy->rkxy/dot_general | solution.py:67
  418.7 2.8 copy.47
  (10 shorter events, 0.6 us)
Async XLA Ops:
  6.5 206.6 %all-gather.2.cloned.1.call-start = ((), (), s32[]{:S(2)}) async-start(), calls=%async_computation.3 | async-start | bytes 17825792 | tf_op jit(solution)/shard_map/all_gather | solution.py:50
  213.2 15.2 %copy-start = (f32[2,64,128,128]{2,1,0,3:T(8,128)S(1)}, f32[2,64,128,128]{2,1,0,3:T(8,128)}, u32[]{:S(2)}) copy-start(f32[2,64,128,128]{2,1,0,3:T(8,128)} %copy.31) | copy-start | bytes 25165828
  245.7 7.0 %copy-start.1 = (bf16[2,64,128,128]{2,1,0,3:T(8,128)(2,1)S(1)}, bf16[2,64,128,128]{2,1,0,3:T(8,128)(2,1)}, u32[]{:S(2)}) copy-start(bf16[2,64,128,128]{2,1,0,3:T(8,128)(2,1)} %get-tuple-element.6) | copy-start | bytes 12582916
Sparse Core Ops, SparseCore 0:
  87.9 125.2 all-gather.1
where the time goes:
time: 436 us; the launch traced here: 429 us
  blocking collectives  148 us (34%)
  local copies, waits for them, and re-layouts  106 us (24%)
  waiting for transfers between devices  95.6 us (22%)
  matrix products  35.9 us (8%)
  other arithmetic  30.2 us (7%)
  between operations  13.7 us (3%)
    all_to_all x1, blocking collectives, body(): lax.all_to_all(planes, 'slab', split_axis=3, concat_axis=2, tiled=True)  97.3 us
    all_gather x1, waiting for transfers between devices, body(): collected = lax.all_gather(pieces, 'grp', axis=1, tiled=True)  95.5 us
    all_to_all x1, blocking collectives, body(): lax.all_to_all(lines.astype(jnp.bfloat16), 'grp', split_axis=1, concat_ax...  31.9 us
    all_to_all x2, local copies, waits for them, and re-layouts, body(): lax.all_to_all(planes, 'slab', split_axis=3, concat_axis=2, tiled=True)  21.4 us
    dot_general x1, matrix products, body(): jnp.einsum('qkn,qrnxy->rkxy', inverse_low[0], lax.all_to_all(planes, 'sla...  21.2 us
    all_to_all x1, blocking collectives, body(): lax.all_to_all(partial_value, 'slab', split_axis=3, concat_axis=4, tiled=...  18.4 us
    reduce_sum x1, other arithmetic, body(): jnp.sum(kernel_real * spec_real - kernel_imag * spec_imag, axis=1)  17.3 us
    slice x1, local copies, waits for them, and re-layouts, body(): spec_real = spec_split[0].astype(jnp.float32)  15.2 us
  transfers between devices with their start and end apart: 1, of which 1 were waited for; matrix products, arithmetic and copies ran while one was open for 7% of the time, Pallas kernels for 0%

commit v1 on v0

--- a/solution.py
+++ b/solution.py
@@ -44,7 +44,12 @@
     pieces = jnp.einsum(
         "pqkn,qyrzn->pyrzk",
         forward_low,
-        lax.all_to_all(partial_value, "slab", split_axis=3, concat_axis=4, tiled=True),
+        jnp.concatenate(
+            lax.all_to_all(
+                jnp.stack(jnp.split(partial_value, lax.axis_size("slab"), axis=3)), "slab", 0, 0
+            ),
+            axis=4,
+        ),
         preferred_element_type=jnp.float32,
     ).astype(jnp.bfloat16)
     collected = lax.all_gather(pieces, "grp", axis=1, tiled=True)

time: 436 us -> 432 us (level)
  local copies, waits for them, and re-layouts: 106 us -> 101 us
    all_to_all x2 -> x0, local copies, waits for them, and re-layouts: 7.4 us -> none  [body(): lax.all_to_all(partial_value, 'slab', split_axis=3, concat_axis=4, tiled=...]
    reshape x0 -> x3, local copies, waits for them, and re-layouts: none -> 7.26 us  [body(): jnp.concatenate(lax.all_to_all(jnp.stack(jnp.split(partial_value, lax.axi...]
    convert_element_type x2 -> x1, local copies, waits for them, and re-layouts: 5.88 us -> 1.06 us  [body(): pieces = jnp.einsum('pqkn,qyrzn->pyrzk', forward_low, jnp.concatenate(lax...]
where the time goes in v1:
time: 432 us; the launch traced here: 424 us
  blocking collectives  148 us (34%)
  local copies, waits for them, and re-layouts  101 us (23%)
  waiting for transfers between devices  95.5 us (22%)
  matrix products  35 us (8%)
  other arithmetic  30.8 us (7%)
  between operations  14 us (3%)
    all_to_all x1, blocking collectives, body(): lax.all_to_all(planes, 'slab', split_axis=3, concat_axis=2, tiled=True)  97.3 us
    all_gather x1, waiting for transfers between devices, body(): collected = lax.all_gather(pieces, 'grp', axis=1, tiled=True)  95.5 us
    all_to_all x1, blocking collectives, body(): lax.all_to_all(lines.astype(jnp.bfloat16), 'grp', split_axis=1, concat_ax...  31.9 us
    all_to_all x2, local copies, waits for them, and re-layouts, body(): lax.all_to_all(planes, 'slab', split_axis=3, concat_axis=2, tiled=True)  21.4 us
    dot_general x1, matrix products, body(): jnp.einsum('qkn,qrnxy->rkxy', inverse_low[0], lax.all_to_all(planes, 'sla...  21.3 us
    all_to_all x1, blocking collectives, body(): lax.all_to_all(jnp.stack(jnp.split(partial_value, lax.axis_size('slab'),...  18.4 us
    reduce_sum x1, other arithmetic, body(): jnp.sum(kernel_real * spec_real - kernel_imag * spec_imag, axis=1)  17.5 us
    slice x1, local copies, waits for them, and re-layouts, body(): spec_real = spec_split[0].astype(jnp.float32)  15.2 us
  transfers between devices with their start and end apart: 1, of which 1 were waited for; matrix products, arithmetic and copies ran while one was open for 7% of the time, Pallas kernels for 0%

profile of v1, /device:TPU:0, one launch (start us, length us, event | category | flops | bytes accessed | tf_op | source)
XLA Modules:
  0.0 424.2 jit_solution(11594017238358159139)
XLA Ops:
  7.1 1.7 fusion.59
  8.8 1.8 bitcast_convert_fusion.6
  10.6 3.0 copy.32
  13.6 1.5 reshape.171
  15.1 31.9 %all_to_all.41 = bf16[16,2,16384]{2,1,0:T(2,128)(2,1)S(1)} all-to-all(bf16[16,2,16384]{2,1,0:T(2,128)(2,1)S(1)} %reshape.171), channel_id=1, replica_groups=mesh['grp'=16,'slab'=2] {'grp'}, dimensions={0} | all-to-all | bytes 2097152 | tf_op jit(solution)/shard_map/all_to_all | solution.py:38
  47.0 1.3 reshape.172
  48.3 2.0 fusion.26
  50.4 0.5 slice_bitcast_fusion.1
  50.9 0.5 fusion.60
  51.3 1.6 reshape.173
  53.0 18.4 %all_to_all.42 = bf16[2,2,131072]{2,1,0:T(2,128)(2,1)} all-to-all(bf16[2,2,131072]{2,1,0:T(2,128)(2,1)S(1)} %reshape.173), channel_id=1, replica_groups=mesh['grp'=16,'slab'=2] {'slab'}, dimensions={0} | all-to-all | bytes 2097152 | tf_op jit(solution)/shard_map/all_to_all | solution.py:48
  71.4 2.6 reshape.174
  74.0 1.5 bitcast_bitcast_fusion
  75.5 4.8 %copy.66 = bf16[2,8,4,64,2,64]{5,4,3,0,2,1:T(2,128)(2,1)S(1)} copy(bf16[2,8,4,64,2,64]{3,5,0,2,1,4:T(8,128)(2,1)} %bitcast_bitcast_fusion) | data formatting | bytes 2097152 | tf_op jit(solution)/shard_map/reshape | solution.py:47
  80.3 1.0 reshape.159
  81.3 0.5 fusion.29
  81.8 1.1 copy.38
  82.8 11.8 %bitcast_convert_fusion.3 = (f32[2,64,128,128]{3,2,1,0:T(8,128)}, f32[2,64,128,128]{3,2,1,0:T(8,128)}) fusion(bf16[1,2,2,64,128,128]{5,4,3,2,1,0:T(8,128)(2,1)} %param.3), kind=kLoop, calls=%fused_computation.25 | loop fusion | flops 4194304 | bytes 25165824 | tf_op jit(solution)/shard_map/convert_element_type | solution.py:59
  94.6 8.8 %copy.31 = f32[2,64,128,128]{2,1,0,3:T(8,128)} copy(f32[2,64,128,128]{3,2,1,0:T(8,128)} %get-tuple-element.9) | data formatting | bytes 16777216 | tf_op jit(solution)/shard_map/convert_element_type | solution.py:59
  103.4 8.8 %copy.39 = f32[2,64,128,128]{2,1,0,3:T(8,128)} copy(f32[2,64,128,128]{3,2,1,0:T(8,128)} %get-tuple-element.10) | data formatting | bytes 16777216 | tf_op jit(solution)/shard_map/convert_element_type | solution.py:60
  112.7 95.5 %all-gather.2.cloned.1.call-done = bf16[2,128,4,64,128]{4,3,2,0,1:T(8,128)(2,1)} async-done(((bf16[2,8,4,64,128]{4,3,2,0,1:T(8,128)(2,1)}), bf16[2,128,4,64,128]{4,3,2,0,1:T(8,128)(2,1)}) %all-gather.2.cloned.1.call-update) | async-done | bytes 16777232 | tf_op jit(solution)/shard_map/all_gather | solution.py:55
  208.3 15.2 %fusion.58 = (bf16[1,4,64,128,128]{3,2,1,0,4:T(8,128)(2,1)}, bf16[1,4,64,128,128]{3,2,1,0,4:T(8,128)(2,1)}) fusion(bf16[2,4,64,128,128]{3,2,1,0,4:T(8,128)(2,1)} %bitcast.150), kind=kLoop, calls=%fused_computation.77 | loop fusion | bytes 33554432 | tf_op jit(solution)/shard_map/slice | solution.py:61
  223.5 17.5 %fusion.1 = (bf16[2,64,128,128]{2,1,0,3:T(8,128)(2,1)}, bf16[2,64,128,128]{2,1,0,3:T(8,128)(2,1)}) fusion(bf16[2,2,64,128,128]{3,2,1,0,4:T(8,128)(2,1)} %bitcast.148, bf16[2,2,64,128,128]{3,2,1,0,4:T(8,128)(2,1)} %bitcast.147, f32[2,64,128,128]{2,1,0,3:T(8,128)} %copy.39, f32[2,64,128,128]{2,1,0,3:T(8,128)S(1)} %copy-done), kind=kLoop, calls=%fused_computation.5 | loop fusion | flops 37748736 | bytes 41943040 | tf_op jit(solution)/shard_map/reduce_sum | solution.py:63
  240.9 7.0 %copy.89 = bf16[2,64,128,128]{2,3,1,0:T(8,128)(2,1)} copy(bf16[2,64,128,128]{2,1,0,3:T(8,128)(2,1)} %get-tuple-element.5) | data formatting | bytes 8388608 | tf_op jit(solution)/shard_map/reduce_sum | solution.py:63
  247.9 4.6 %copy.90 = bf16[2,64,128,128]{2,3,1,0:T(8,128)(2,1)} copy(bf16[2,64,128,128]{2,1,0,3:T(8,128)(2,1)S(1)} %copy-done.1) | data formatting | bytes 8388608 | tf_op jit(solution)/shard_map/reduce_sum | solution.py:64
  252.6 9.3 %fusion.7 = bf16[2,2,64,128,128]{4,3,0,2,1:T(8,128)(2,1)} fusion(bf16[1,2,64,128,128]{3,4,0,2,1:T(8,128)(2,1)} %bitcast.154, bf16[1,2,64,128,128]{3,4,0,2,1:T(8,128)(2,1)} %bitcast.153, bf16[1,2,128,128]{3,2,1,0:T(8,128)(2,1)S(1)} %get-tuple-element.18, bf16[1,2,128,128]{3,2,1,0:T(8,128)(2,1)S(1)} %get-tuple-element.17), kind=kOutput, calls=%fused_computation.12 | convolution fusion | flops 4320657408 | bytes 16908288 | tf_op jit(solution)/shard_map/pqkn,qrzxn->przxk/dot_general | solution.py:69
  261.9 12.2 %copy.43 = bf16[2,2,64,128,128]{4,0,2,1,3:T(2,128)(2,1)S(1)} copy(bf16[2,2,64,128,128]{4,3,0,2,1:T(8,128)(2,1)} %fusion.7) | data formatting | bytes 16777216 | tf_op jit(solution)/shard_map/convert_element_type | solution.py:71
  274.1 97.3 %all_to_all.43 = bf16[2,2,64,128,128]{4,0,2,1,3:T(2,128)(2,1)} all-to-all(bf16[2,2,64,128,128]{4,0,2,1,3:T(2,128)(2,1)S(1)} %copy.43), channel_id=1, replica_groups=mesh['grp'=16,'slab'=2] {'slab'}, dimensions={3} | all-to-all | bytes 16777216 | tf_op jit(solution)/shard_map/all_to_all | solution.py:75
  371.5 12.0 %copy.44 = bf16[2,2,64,128,128]{4,3,2,1,0:T(8,128)(2,1)} copy(bf16[2,2,64,128,128]{4,0,2,1,3:T(2,128)(2,1)} %all_to_all.43) | data formatting | bytes 16777216 | tf_op jit(solution)/shard_map/all_to_all | solution.py:75
  383.5 9.4 %copy.45 = bf16[2,2,2,64,64,128]{5,4,3,2,1,0:T(8,128)(2,1)} copy(bf16[2,2,2,64,64,128]{5,4,2,3,1,0:T(8,128)(2,1)} %bitcast.149) | data formatting | bytes 16777216 | tf_op jit(solution)/shard_map/all_to_all | solution.py:75
  392.8 21.3 %bitcast_reduce_fusion = bf16[64,128,128]{2,1,0:T(8,128)(2,1)S(1)} fusion(bf16[2,2,128,64,128]{4,3,2,1,0:T(8,128)(2,1)} %bitcast.152, bf16[1,128,128]{2,1,0:T(8,128)(2,1)S(1)} %get-tuple-element.22, bf16[1,128,128]{2,1,0:T(8,128)(2,1)S(1)} %fusion.51), kind=kOutput, calls=%fused_computation.17 | convolution fusion | flops 1074823168 | bytes 10551296 | tf_op jit(solution)/shard_map/qkn,qrnxy->rkxy/dot_general | solution.py:72
  414.2 2.8 copy.47
  (12 shorter events, 1.1 us)
Async XLA Ops:
  6.5 201.7 %all-gather.2.cloned.1.call-start = ((), (), s32[]{:S(2)}) async-start(), calls=%async_computation.3 | async-start | bytes 17825792 | tf_op jit(solution)/shard_map/all_gather | solution.py:55
  208.3 15.2 %copy-start = (f32[2,64,128,128]{2,1,0,3:T(8,128)S(1)}, f32[2,64,128,128]{2,1,0,3:T(8,128)}, u32[]{:S(2)}) copy-start(f32[2,64,128,128]{2,1,0,3:T(8,128)} %copy.31) | copy-start | bytes 25165828
  240.9 7.0 %copy-start.1 = (bf16[2,64,128,128]{2,1,0,3:T(8,128)(2,1)S(1)}, bf16[2,64,128,128]{2,1,0,3:T(8,128)(2,1)}, u32[]{:S(2)}) copy-start(bf16[2,64,128,128]{2,1,0,3:T(8,128)(2,1)} %get-tuple-element.6) | copy-start | bytes 12582916
Sparse Core Ops, SparseCore 0:
  83.0 125.2 all-gather.1
